TPU v7x, 32 devices: a whole 2x2x4 slice. The times are simulated.
32 devices in a mesh: grating: 2 (over x), layer: 4 (over z), harm: 4 (over y, core).
Axes of the slice: x: 2, y: 2, z: 4, core: 2. Of those that a mesh axis runs over, the one named last changes fastest.
Arguments:
- panels: float32 [8, 1280, 2, 640], P(('grating', 'layer'), 'harm'), parts along dimension 0, may hold values from -6 to 6
- factors: float32 [16, 1280, 2, 1280], P(('grating', 'layer'), 'harm'), parts along dimension 0, may hold values from -0.25 to 0.25
- decay: float32 [16, 1280], P(('grating', 'layer'), 'harm'), parts along dimension 0, may hold values from 0.25 to 1
- phase: float32 [16, 1280], P(('grating', 'layer'), 'harm'), parts along dimension 0, may hold values from -3.140625 to 3.140625
- kept: int32 [16], P(('grating', 'layer')), parts along dimension 0, may hold values from 640 to 1280
- start: int32 [8], P(('grating', 'layer')), parts along dimension 0, may hold values from 0 to 1
Outputs:
- advanced: float32 [8, 1280, 2, 640], P(('grating', 'layer'), 'harm'), parts along dimension 0
There are 2 independent parts, one for each index of `grating`. A program takes and returns all parts, laid end to end along the dimension named above; each array names one. Nothing has to cross between parts.
All inputs are finite; a program needn't handle non-finite values.
Results may differ from a plain program's by a relative error of at most 0.00024.
Values sent between devices are 32-bit elements; how exact they have to be, the bound alone decides.
A program may use at most 128 MiB of HBM per device.

v0:
```python
import jax
import jax.numpy as jnp
from jax import lax
from jax.sharding import PartitionSpec as P


def shifted(block, axis, distance):
    devices = range(lax.axis_size(axis))
    route = [((i - distance) % len(devices), i) for i in devices]
    return lax.ppermute(block, axis, route)


def contract(left_matrix, right_matrix):
    return lax.dot_general(
        left_matrix,
        right_matrix,
        (((0,), (0,)), ((), ())),
        precision=lax.Precision.HIGHEST,
        preferred_element_type=jnp.float32,
    )


def propagate(block, magnitude, angles):
    prop_real = (magnitude * jnp.cos(angles))[:, None]
    prop_imag = (magnitude * jnp.sin(angles))[:, None]
    real_in = prop_real * block[:, 0] - prop_imag * block[:, 1]
    imag_in = prop_real * block[:, 1] + prop_imag * block[:, 0]
    return (real_in, imag_in)


def complex_apply(real_block, imag_block, real_in, imag_in):
    real_out = contract(real_block, real_in) - contract(imag_block, imag_in)
    imag_out = contract(real_block, imag_in) + contract(imag_block, real_in)
    return jnp.stack([real_out, imag_out], 1)


def make_partial(factor_block, real_in, imag_in):
    real_block = factor_block[:, 0]
    imag_block = factor_block[:, 1]
    return complex_apply(real_block, imag_block, real_in, imag_in)


def on_device(panels, factors, decay, phase, kept, start):
    group_layers = factors.shape[0]
    local_rows = factors.shape[1]
    harmonic_index = lax.axis_index("harm") * local_rows + lax.iota(jnp.int32, local_rows)
    current = panels[0]
    for section_step in range(group_layers):
        layer_id = (start[0] + section_step) % group_layers
        factor_block = lax.dynamic_index_in_dim(factors, layer_id, 0, keepdims=False)
        live_rows = (harmonic_index < kept[layer_id]).astype(jnp.float32)
        magnitude = lax.dynamic_index_in_dim(decay, layer_id, 0, keepdims=False) * live_rows
        angles = lax.dynamic_index_in_dim(phase, layer_id, 0, keepdims=False)
        real_in, imag_in = propagate(current, magnitude, angles)
        current = lax.psum_scatter(
            make_partial(factor_block, real_in, imag_in), "harm", scatter_dimension=0, tiled=True
        )
    handed = shifted(current, "layer", 1)
    return handed[None]


def solution(mesh):
    in_specs = (
        P(("grating", "layer"), "harm", None, None),
        P(("grating", "layer"), "harm", None, None),
        P(("grating", "layer"), "harm"),
        P(("grating", "layer"), "harm"),
        P(("grating", "layer")),
        P(("grating", "layer")),
    )
    out_specs = P(("grating", "layer"), "harm", None, None)
    return jax.shard_map(
        on_device, mesh=mesh, in_specs=in_specs, out_specs=out_specs, check_vma=False
    )
```

profile of v0, /device:TPU:0, one launch (start us, length us, event | category | flops | bytes accessed | tf_op | source)
XLA Modules:
  0.0 256.3 jit_solution(6656093142292069415)
XLA Ops:
  6.5 0.0 reduce-scatter.3.cloned.1.call-start
  7.2 1.4 fusion.46
  8.6 6.9 %dynamic-slice_bitcast_fusion = (f32[320,2,1280]{2,1,0:T(2,128)S(1)}, f32[320,2,1280]{2,1,0:T(2,128)}) fusion(f32[2,320,2,1280]{3,2,1,0:T(2,128)} %param.7, s32[]{:T(128)S(6)} %select_n.28, s32[]{:T(128)S(6)} %select_n.26), kind=kLoop, calls=%fused_computation.10 | loop fusion | bytes 13107208 | tf_op jit(solution)/shard_map/jit(dynamic_index_in_dim)/squeeze | solution.py:50
  15.6 0.0 copy-start.1
  15.6 0.0 copy-start.2
  15.6 2.5 fusion.45
  18.1 0.0 copy-done.1
  18.1 0.0 copy-done.2
  18.1 0.1 cosine_reduce_fusion.1
  18.2 0.7 fusion.41
  18.9 4.4 %multiply_subtract_fusion.1 = (f32[320,1,640]{2,1,0:T(1,128)S(1)}, f32[320,1,640]{2,1,0:T(1,128)S(1)}) fusion(f32[320,2,640]{2,1,0:T(2,128)} %bitcast.61, f32[320]{0:T(512)S(1)} %get-tuple-element.22, f32[320]{0:T(512)S(1)} %get-tuple-element.21), kind=kLoop, calls=%fused_computation.43 | loop fusion | flops 1228800 | bytes 3279360 | tf_op jit(solution)/shard_map/sub | solution.py:26
  23.3 6.2 %fusion.8 = f32[1280,640]{1,0:T(8,128)S(1)} fusion(f32[320,1,1280]{2,1,0:T(1,128)S(1)} %get-tuple-element.16, f32[320,1,640]{2,1,0:T(1,128)S(1)} %get-tuple-element.18), kind=kOutput, calls=%fused_computation.16 | convolution fusion | flops 3145728000 | bytes 5734400 | tf_op jit(solution)/shard_map/dot_general | solution.py:14
  29.5 6.7 %fusion.10 = f32[1280,640]{1,0:T(8,128)S(1)} fusion(f32[320,1,1280]{2,1,0:T(1,128)S(1)} %get-tuple-element.16, f32[320,1,640]{2,1,0:T(1,128)S(1)} %get-tuple-element.17), kind=kOutput, calls=%fused_computation.18 | convolution fusion | flops 3145728000 | bytes 5734400 | tf_op jit(solution)/shard_map/dot_general | solution.py:14
  36.2 6.3 %fusion.1 = f32[1280,1,640]{2,0,1:T(8,128)S(1)} fusion(f32[1280,640]{1,0:T(8,128)S(1)} %fusion.8, f32[320,1,1280]{2,1,0:T(1,128)S(1)} %get-tuple-element.15, f32[320,1,640]{2,1,0:T(1,128)S(1)} %get-tuple-element.17), kind=kOutput, calls=%fused_computation.7 | convolution fusion | flops 3146547200 | bytes 9011200 | tf_op jit(solution)/shard_map/dot_general | solution.py:14
  42.6 6.5 %fusion = f32[1280,1,640]{2,0,1:T(8,128)S(1)} fusion(f32[1280,640]{1,0:T(8,128)S(1)} %fusion.10, f32[320,1,1280]{2,1,0:T(1,128)S(1)} %get-tuple-element.15, f32[320,1,640]{2,1,0:T(1,128)S(1)} %get-tuple-element.18), kind=kOutput, calls=%fused_computation.6 | convolution fusion | flops 3146547200 | bytes 9011200 | tf_op jit(solution)/shard_map/dot_general | solution.py:14
  49.0 3.2 %pad_maximum_fusion = f32[1280,2,640]{2,0,1:T(8,128)} fusion(f32[1280,1,640]{2,0,1:T(8,128)S(1)} %fusion.1, f32[1280,1,640]{2,0,1:T(8,128)S(1)} %fusion), kind=kLoop, calls=%fused_computation | loop fusion | flops 1638400 | bytes 13107200 | tf_op jit(solution)/shard_map/stack | solution.py:34
  52.2 0.0 reduce-scatter.3.cloned.1.call-update
  52.2 0.0 reduce-scatter.5.cloned.1.call-start
  52.3 0.7 fusion.43
  52.9 5.7 %fusion.44 = (f32[320,1,1280]{2,1,0:T(1,128)S(1)}, f32[320,1,1280]{2,1,0:T(1,128)S(1)}) fusion(f32[320,2,1280]{2,1,0:T(2,128)} %get-tuple-element.12), kind=kLoop, calls=%fused_computation.65 | loop fusion | bytes 6553600 | tf_op jit(solution)/shard_map/slice | solution.py:39
  58.7 57.1 %reduce-scatter.3.cloned.1.call-done = f32[320,2,640]{2,0,1:T(8,128)} async-done(((f32[1280,2,640]{2,0,1:T(8,128)}), f32[320,2,640]{2,0,1:T(8,128)}) %reduce-scatter.3.cloned.1.call-update) | async-done | bytes 1638416 | tf_op jit(solution)/shard_map/reduce_scatter | solution.py:55
  115.7 7.8 %fusion.12 = f32[1280,640]{1,0:T(8,128)S(1)} fusion(f32[320,1,1280]{2,1,0:T(1,128)S(1)} %get-tuple-element.14, f32[320,2,640]{2,0,1:T(8,128)} %reduce-scatter.3.cloned.1.call-done, f32[320]{0:T(512)S(1)} %get-tuple-element.20, f32[320]{0:T(512)S(1)} %get-tuple-element.19), kind=kOutput, calls=%fused_computation.20 | convolution fusion | flops 3146342400 | bytes 6556160 | tf_op jit(solution)/shard_map/dot_general | solution.py:14
  123.6 0.0 copy-done
  123.6 6.5 %fusion.14 = f32[1280,640]{1,0:T(8,128)S(1)} fusion(f32[320,1,1280]{2,1,0:T(1,128)S(1)} %get-tuple-element.14, f32[320,2,640]{2,0,1:T(8,128)S(1)} %copy-done, f32[320]{0:T(512)S(1)} %get-tuple-element.20, f32[320]{0:T(512)S(1)} %get-tuple-element.19), kind=kOutput, calls=%fused_computation.22 | convolution fusion | flops 3146342400 | bytes 6556160 | tf_op jit(solution)/shard_map/dot_general | solution.py:14
  130.1 6.4 %fusion.3 = f32[1280,1,640]{2,0,1:T(8,128)S(1)} fusion(f32[1280,640]{1,0:T(8,128)S(1)} %fusion.12, f32[320,1,1280]{2,1,0:T(1,128)S(1)} %get-tuple-element.13, f32[320,2,640]{2,0,1:T(8,128)S(1)} %copy-done, f32[320]{0:T(512)S(1)} %get-tuple-element.20, f32[320]{0:T(512)S(1)} %get-tuple-element.19), kind=kOutput, calls=%fused_computation.9 | convolution fusion | flops 3147161600 | bytes 9832960 | tf_op jit(solution)/shard_map/dot_general | solution.py:14
  136.5 6.7 %fusion.2 = f32[1280,1,640]{2,0,1:T(8,128)S(1)} fusion(f32[1280,640]{1,0:T(8,128)S(1)} %fusion.14, f32[320,1,1280]{2,1,0:T(1,128)S(1)} %get-tuple-element.13, f32[320,2,640]{2,0,1:T(8,128)S(1)} %copy-done, f32[320]{0:T(512)S(1)} %get-tuple-element.20, f32[320]{0:T(512)S(1)} %get-tuple-element.19), kind=kOutput, calls=%fused_computation.8 | convolution fusion | flops 3147161600 | bytes 9832960 | tf_op jit(solution)/shard_map/dot_general | solution.py:14
  143.2 3.2 %pad_maximum_fusion.1 = f32[1280,2,640]{2,0,1:T(8,128)} fusion(f32[1280,1,640]{2,0,1:T(8,128)S(1)} %fusion.3, f32[1280,1,640]{2,0,1:T(8,128)S(1)} %fusion.2), kind=kLoop, calls=%fused_computation.1 | loop fusion | flops 1638400 | bytes 13107200 | tf_op jit(solution)/shard_map/stack | solution.py:34
  146.4 0.0 reduce-scatter.5.cloned.1.call-update
  146.4 60.8 %reduce-scatter.5.cloned.1.call-done = f32[320,2,640]{2,0,1:T(8,128)} async-done(((f32[1280,2,640]{2,0,1:T(8,128)}), f32[320,2,640]{2,0,1:T(8,128)}) %reduce-scatter.5.cloned.1.call-update) | async-done | bytes 1638416 | tf_op jit(solution)/shard_map/reduce_scatter | solution.py:55
  207.2 1.5 collective-permute-start
  208.7 37.9 %collective-permute-done = f32[320,2,640]{2,0,1:T(8,128)S(1)} collective-permute-done((f32[320,2,640]{2,0,1:T(8,128)}, f32[320,2,640]{2,0,1:T(8,128)S(1)}, u32[]{:S(2)}, u32[]{:S(2)}) %collective-permute-start) | collective-permute-done | bytes 1638432 | tf_op jit(solution)/shard_map/ppermute | solution.py:10
  246.6 2.4 copy.7
  (1 shorter events, 0.0 us)
Async XLA Ops:
  6.5 109.2 %reduce-scatter.3.cloned.1.call-start = ((), (), s32[]{:S(2)}) async-start(), calls=%async_computation.2 | async-start | bytes 8192000 | tf_op jit(solution)/shard_map/reduce_scatter | solution.py:55
  15.6 2.5 copy-start.1
  15.6 2.5 copy-start.2
  52.2 154.9 %reduce-scatter.5.cloned.1.call-start = ((), (), s32[]{:S(2)}) async-start(), calls=%async_computation.3 | async-start | bytes 8192000 | tf_op jit(solution)/shard_map/reduce_scatter | solution.py:55
  115.7 7.8 %copy-start = (f32[320,2,640]{2,0,1:T(8,128)S(1)}, f32[320,2,640]{2,0,1:T(8,128)}, u32[]{:S(2)}) copy-start(f32[320,2,640]{2,0,1:T(8,128)} %reduce-scatter.3.cloned.1.call-done) | copy-start | bytes 4915204
  207.2 39.4 %collective-permute-start = (f32[320,2,640]{2,0,1:T(8,128)}, f32[320,2,640]{2,0,1:T(8,128)S(1)}, u32[]{:S(2)}, u32[]{:S(2)}) collective-permute-start(f32[320,2,640]{2,0,1:T(8,128)} %reduce-scatter.5.cloned.1.call-done), channel_id=1, source_target_pairs={{12,0},{0,4},{4,8},{8,12},{13,1},{1,5},{5,9},{9,13},{14,2},{2,6},{... | collective-permute-start | bytes 4915208 | tf_op jit(solution)/shard_map/ppermute | solution.py:10
Sparse Core Ops, SparseCore 0:
  52.4 63.3 reduce-scatter.2
  146.5 60.6 reduce-scatter.4
where the time goes:
time: 261 us; the launch traced here: 256 us
  waiting for transfers between devices  156 us (60%)
  matrix products  53.1 us (20%)
  local copies, waits for them, and re-layouts  19.2 us (7%)
  between operations  14.7 us (6%)
  other arithmetic  12 us (5%)
    reduce_scatter x2, waiting for transfers between devices, on_device(): lax.psum_scatter(make_partial(factor_block, real_in, imag_in), 'harm', sc...  118 us
    dot_general x8, matrix products, contract(): lax.dot_general(left_matrix, right_matrix, (((0,), (0,)), ((), ())), prec...  53.1 us
    ppermute x1, waiting for transfers between devices, shifted(): return lax.ppermute(block, axis, route)  37.9 us
    slice x2, local copies, waits for them, and re-layouts, make_partial(): imag_block = factor_block[:, 1]  8.26 us
    squeeze x1, local copies, waits for them, and re-layouts, on_device(): lax.dynamic_index_in_dim(factors, layer_id, 0, keepdims=False)  6.92 us
    another operation x2, other arithmetic, complex_apply(): return jnp.stack([real_out, imag_out], 1)  6.31 us
  transfers between devices with their start and end apart: 3, of which 3 were waited for; matrix products, arithmetic and copies ran while one was open for 2% of the time, Pallas kernels for 0%

commit v1 on v0

v1 whole, which is shorter than its diff:
```python
import functools

import jax
import jax.numpy as jnp
from jax import lax
from jax.experimental import pallas as pl
from jax.experimental.layout import Layout, with_layout_constraint
from jax.experimental.pallas import tpu as pltpu
from jax.sharding import PartitionSpec as P

LANES = 128
CORES = 2
MESH = pl.DeviceIdType.MESH


def split(value):
    high = value.astype(jnp.bfloat16)
    low = (value - high.astype(jnp.float32)).astype(jnp.bfloat16)
    return high, low


def kernel(
    steps, chips, groups, rows, harmonics, chunks, depth,
    start_ref, kept_ref, decay_ref, phase_ref, panel_ref, factor_ref, out_ref,
    matrix, right, prop, own, sib_send, sib_recv, keep, far_send, far_recv, next_send,
    sib_ss, sib_rs, far_ss, far_rs, next_ss, next_rs,
):
    harm = lax.axis_index("harm")
    layer = lax.axis_index("layer")
    chip, core = harm // CORES, lax.rem(harm, CORES)
    other = 1 - core
    sibling = {"harm": chip * CORES + other}
    after = {"layer": lax.rem(layer + 1, groups)}
    before = {"layer": lax.rem(layer + groups - 1, groups)}
    width = 2 * LANES
    tiles = harmonics // LANES

    def far_chip(distance):
        return lax.rem(chip + distance, chips)

    def far_device(distance):
        return {"harm": far_chip(distance) * CORES + core}

    barrier = pltpu.get_barrier_semaphore()
    friends = [sibling, after, before] + [far_device(d) for d in range(1, chips)]
    for friend in friends:
        pl.semaphore_signal(barrier, inc=1, device_id=friend, device_id_type=MESH)

    def sib_copy(step, q):
        return pltpu.make_async_remote_copy(
            src_ref=sib_send.at[step, q], dst_ref=sib_recv.at[step, q],
            send_sem=sib_ss.at[step, q], recv_sem=sib_rs.at[step, q],
            device_id=sibling, device_id_type=MESH,
        )

    def far_copy(step, q, distance):
        return pltpu.make_async_remote_copy(
            src_ref=far_send.at[step, q, distance - 1],
            dst_ref=far_recv.at[step, q, distance - 1],
            send_sem=far_ss.at[step, q, distance - 1],
            recv_sem=far_rs.at[step, q, distance - 1],
            device_id=far_device(distance), device_id_type=MESH,
        )

    def next_copy(q):
        return pltpu.make_async_remote_copy(
            src_ref=next_send.at[q], dst_ref=out_ref.at[q],
            send_sem=next_ss.at[q], recv_sem=next_rs.at[q],
            device_id=after, device_id_type=MESH,
        )

    def load_matrix(step):
        base = lax.rem(start_ref[0] + step, steps) * (rows * tiles * 2)

        def one(tile, carry):
            first = base + tile * 2
            real = factor_ref[pl.ds(first, rows, stride=tiles * 2), :]
            imag = factor_ref[pl.ds(first + 1, rows, stride=tiles * 2), :]
            high, low = split(jnp.concatenate([real, imag], 0).T)
            here = pl.ds(pl.multiple_of(tile * LANES, LANES), LANES)
            matrix[step, here, 0:2 * rows] = high
            matrix[step, here, depth:depth + 2 * rows] = high
            matrix[step, here, 2 * depth:2 * depth + 2 * rows] = low
            return carry

        lax.fori_loop(0, tiles, one, 0)

    def propagator(step):
        layer_id = lax.rem(start_ref[0] + step, steps)
        index = harm * rows + lax.broadcasted_iota(jnp.int32, (1, rows), 1)
        live = (index < kept_ref[layer_id]).astype(jnp.float32)
        magnitude = decay_ref[pl.ds(layer_id, 1), :] * live
        angles = phase_ref[pl.ds(layer_id, 1), :]
        for part, line in enumerate((magnitude * jnp.cos(angles), magnitude * jnp.sin(angles))):
            prop[step, part] = jnp.broadcast_to(line, (LANES, rows)).T

    def load_right(step, real, imag):
        prop_real, prop_imag = prop[step, 0], prop[step, 1]
        high_r, low_r = split(prop_real * real - prop_imag * imag)
        high_i, low_i = split(prop_real * imag + prop_imag * real)
        for place, r, i in ((0, high_r, high_i), (depth, low_r, low_i), (2 * depth, high_r, high_i)):
            right[place:place + rows, 0:LANES] = r
            right[place:place + rows, LANES:width] = i
            right[place + rows:place + 2 * rows, 0:LANES] = -i
            right[place + rows:place + 2 * rows, LANES:width] = r

    def block(index):
        return pl.ds(pl.multiple_of(index * rows, rows), rows)

    def product(step, index):
        return jnp.dot(
            matrix[step, block(index), :], right[...], preferred_element_type=jnp.float32
        )

    def contribute(step, q):
        def give(place, carry):
            sib_send[step, q, block(place), :] = product(step, place * CORES + other)
            return carry

        lax.fori_loop(0, chips, give, 0)
        sib_copy(step, q).start()

        def hold(place, carry):
            own[block(place), :] = product(step, place * CORES + core)
            return carry

        lax.fori_loop(0, chips, hold, 0)
        sib_copy(step, q).wait_recv()
        for distance in range(1, chips):
            there = block(far_chip(distance))
            far_send[step, q, distance - 1] = own[there, :] + sib_recv[step, q, there, :]
            far_copy(step, q, distance).start()
        mine = block(chip)
        keep[step, q] = own[mine, :] + sib_recv[step, q, mine, :]

    def collect(step, q):
        total = keep[step, q]
        for distance in range(1, chips):
            far_copy(step, q, distance).wait_recv()
            total = total + far_recv[step, q, distance - 1]
        return total

    if depth > 2 * rows:
        matrix[...] = jnp.zeros_like(matrix)
        right[...] = jnp.zeros_like(right)

    for step in range(steps):
        propagator(step)
    load_matrix(0)
    pl.semaphore_wait(barrier, len(friends))

    def enter(q, carry):
        first = q * 2
        load_right(
            0,
            panel_ref[pl.ds(first, rows, stride=chunks * 2), :],
            panel_ref[pl.ds(first + 1, rows, stride=chunks * 2), :],
        )
        contribute(0, q)
        return carry

    lax.fori_loop(0, chunks, enter, 0)

    for step in range(1, steps):
        load_matrix(step)

        def advance(q, carry, step=step):
            total = collect(step - 1, q)
            load_right(step, total[:, 0:LANES], total[:, LANES:width])
            contribute(step, q)
            return carry

        lax.fori_loop(0, chunks, advance, 0)

    def leave(q, carry):
        next_send[q] = collect(steps - 1, q)
        next_copy(q).start()
        return carry

    lax.fori_loop(0, chunks, leave, 0)

    def finish(q, carry):
        for step in range(steps):
            sib_copy(step, q).wait_send()
            for distance in range(1, chips):
                far_copy(step, q, distance).wait_send()
        next_copy(q).wait()
        return carry

    lax.fori_loop(0, chunks, finish, 0)


def lines(array):
    lead = array.shape[:-1]
    tiles = array.shape[-1] // LANES
    split_up = array.reshape(-1, lead[-1], tiles, LANES)
    split_up = with_layout_constraint(split_up, Layout(major_to_minor=(0, 2, 1, 3)))
    return split_up.transpose(0, 2, 1, 3).reshape(-1, LANES)


def on_device(panels, factors, decay, phase, kept, start):
    steps, rows, _, harmonics = factors.shape
    columns = panels.shape[-1]
    chips = lax.axis_size("harm") // CORES
    groups = lax.axis_size("layer")
    chunks = columns // LANES
    depth = -(-2 * rows // LANES) * LANES
    width = 2 * LANES

    vmem = pl.BlockSpec(memory_space=pltpu.VMEM)
    smem = pl.BlockSpec(memory_space=pltpu.SMEM)
    dma = pltpu.SemaphoreType.DMA
    far = max(chips - 1, 1)
    result = pl.pallas_call(
        functools.partial(kernel, steps, chips, groups, rows, harmonics, chunks, depth),
        out_shape=jax.ShapeDtypeStruct((chunks, rows, width), jnp.float32),
        in_specs=[smem, smem, vmem, vmem, vmem, vmem],
        out_specs=vmem,
        scratch_shapes=[
            pltpu.VMEM((steps, harmonics, 3 * depth), jnp.bfloat16),
            pltpu.VMEM((3 * depth, width), jnp.bfloat16),
            pltpu.VMEM((steps, 2, rows, LANES), jnp.float32),
            pltpu.VMEM((chips * rows, width), jnp.float32),
            pltpu.VMEM((steps, chunks, chips * rows, width), jnp.float32),
            pltpu.VMEM((steps, chunks, chips * rows, width), jnp.float32),
            pltpu.VMEM((steps, chunks, rows, width), jnp.float32),
            pltpu.VMEM((steps, chunks, far, rows, width), jnp.float32),
            pltpu.VMEM((steps, chunks, far, rows, width), jnp.float32),
            pltpu.VMEM((chunks, rows, width), jnp.float32),
            dma((steps, chunks)),
            dma((steps, chunks)),
            dma((steps, chunks, far)),
            dma((steps, chunks, far)),
            dma((chunks,)),
            dma((chunks,)),
        ],
        compiler_params=pltpu.CompilerParams(
            collective_id=0, has_side_effects=True, vmem_limit_bytes=60 * 2**20
        ),
    )(start, kept, decay, phase, lines(panels), lines(factors))
    result = result.reshape(chunks, rows, 2, LANES).transpose(1, 2, 0, 3)
    result = with_layout_constraint(result, Layout(major_to_minor=(0, 2, 1, 3)))
    return result.reshape(panels.shape)


def solution(mesh):
    in_specs = (
        P(("grating", "layer"), "harm", None, None),
        P(("grating", "layer"), "harm", None, None),
        P(("grating", "layer"), "harm"),
        P(("grating", "layer"), "harm"),
        P(("grating", "layer")),
        P(("grating", "layer")),
    )
    out_specs = P(("grating", "layer"), "harm", None, None)
    return jax.shard_map(
        on_device, mesh=mesh, in_specs=in_specs, out_specs=out_specs, check_vma=False
    )
```

time: 261 us -> 101 us (0.39); the launches traced: 256 us -> 101 us
  waiting for transfers between devices: 156 us -> 0 us
  Pallas kernels: 0 us -> 96.1 us
  matrix products: 53.1 us -> 0 us
  local copies, waits for them, and re-layouts: 19.2 us -> 3.82 us
  between operations: 14.7 us -> 0.67 us
  other arithmetic: 12 us -> 0 us
    reduce_scatter x2 -> x0, waiting for transfers between devices: 118 us -> none  [on_device(): lax.psum_scatter(make_partial(factor_block, real_in, imag_in), 'harm', sc...]
    pallas_call x0 -> x1, Pallas kernels: none -> 96.1 us  [on_device(): pl.pallas_call(functools.partial(kernel, steps, chips, groups, rows, harm...]
    dot_general x8 -> x0, matrix products: 53.1 us -> none  [contract(): lax.dot_general(left_matrix, right_matrix, (((0,), (0,)), ((), ())), prec...]
    ppermute x1 -> x0, waiting for transfers between devices: 37.9 us -> none  [shifted(): return lax.ppermute(block, axis, route)]
    slice x2 -> x0, local copies, waits for them, and re-layouts: 8.26 us -> none  [make_partial(): imag_block = factor_block[:, 1]]
    squeeze x1 -> x0, local copies, waits for them, and re-layouts: 6.92 us -> none  [on_device(): lax.dynamic_index_in_dim(factors, layer_id, 0, keepdims=False)]
    another operation x2 -> x0, other arithmetic: 6.31 us -> none  [complex_apply(): return jnp.stack([real_out, imag_out], 1)]
    sub x1 -> x0, other arithmetic: 4.38 us -> none  [propagate(): real_in = prop_real * block[:, 0] - prop_imag * block[:, 1]]
  transfers between devices with their start and end apart: 3 -> 0, of which waited for: 3 -> 0; matrix products, arithmetic and copies ran while one was open for 2% -> 0% of each run, Pallas kernels for 0% -> 0%
where the time goes in v1:
time: 101 us
  Pallas kernels  96.1 us (95%)
  local copies, waits for them, and re-layouts  3.82 us (4%)
    pallas_call x1, Pallas kernels, on_device(): pl.pallas_call(functools.partial(kernel, steps, chips, groups, rows, harm...  96.1 us
    reshape x2, local copies, waits for them, and re-layouts, on_device(): result = result.reshape(chunks, rows, 2, LANES).transpose(1, 2, 0, 3)  3.82 us

profile of v1, /device:TPU:0, one launch (start us, length us, event | category | flops | bytes accessed | tf_op | source)
XLA Modules:
  0.0 100.6 jit_solution(4937485126231345967)
XLA Ops:
  0.7 96.1 %shard_map.64 = f32[5,320,256]{2,1,0:T(8,128)} custom-call(s32[1]{0:T(128)S(6)} %copy.11.start_ref, s32[2]{0:T(128)} %kept_ref.1, f32[2,320]{1,0:T(2,128)} %decay_ref.1, f32[2,320]{1,0:T(2,128)} %phase_ref.1, f32[3200,128]{1,0:T(8,128)} %bitcast.16, f32[12800,128]{1,0:T(8,128)} %bitcast.15), custom_call_target="tpu_custom_call" | custom-call | tf_op jit(solution)/shard_map/pallas_call | solution.py:214
  96.8 2.1 %reshape.22 = f32[5,320,2,128]{3,2,1,0:T(2,128)S(1)} reshape(f32[5,320,256]{2,1,0:T(8,128)} %shard_map.64) | data formatting | bytes 3276800 | tf_op jit(solution)/shard_map/reshape | solution.py:241
  98.9 1.7 %copy.10 = f32[5,320,2,128]{3,2,0,1:T(2,128)} copy(f32[5,320,2,128]{3,2,1,0:T(2,128)S(1)} %reshape.22) | data formatting | bytes 3276800 | tf_op jit(solution)/shard_map/reshape | solution.py:241

commit v2 on v1

v2 whole, which is shorter than its diff:
```python
import functools

import jax
import jax.numpy as jnp
from jax import lax
from jax.experimental import pallas as pl
from jax.experimental.layout import Layout, with_layout_constraint
from jax.experimental.pallas import tpu as pltpu
from jax.sharding import PartitionSpec as P

LANES = 128
CORES = 2
MESH = pl.DeviceIdType.MESH


def split(value):
    high = value.astype(jnp.bfloat16)
    low = (value - high.astype(jnp.float32)).astype(jnp.bfloat16)
    return high, low


def kernel(
    steps, chips, groups, rows, harmonics, chunks, depth, pieces,
    start_ref, kept_ref, decay_ref, phase_ref, panel_hbm, factor_hbm, out_hbm,
    panel_ref, factor_ref, out_ref,
    matrix, right, prop, own, sib_send, sib_recv, keep, far_send, far_recv, next_send, next_recv,
    in_sem, out_sem, sib_ss, sib_rs, far_ss, far_rs, next_ss, next_rs,
):
    harm = lax.axis_index("harm")
    layer = lax.axis_index("layer")
    chip, core = harm // CORES, lax.rem(harm, CORES)
    other = 1 - core
    sibling = {"harm": chip * CORES + other}
    after = {"layer": lax.rem(layer + 1, groups)}
    before = {"layer": lax.rem(layer + groups - 1, groups)}
    width = 2 * LANES
    tiles = harmonics // LANES
    piece_rows = rows // pieces
    out_rows = piece_rows * chunks * 2

    def far_chip(distance):
        return lax.rem(chip + distance, chips)

    def far_device(distance):
        return {"harm": far_chip(distance) * CORES + core}

    panel_copy = pltpu.make_async_copy(panel_hbm, panel_ref, in_sem.at[0])
    panel_copy.start()
    share = rows * tiles * 2
    factor_copies = [
        pltpu.make_async_copy(
            factor_hbm.at[pl.ds(part * share, share), :],
            factor_ref.at[pl.ds(part * share, share), :],
            in_sem.at[1 + part],
        )
        for part in range(steps)
    ]
    for copy in factor_copies:
        copy.start()

    barrier = pltpu.get_barrier_semaphore()
    friends = [sibling, after, before] + [far_device(d) for d in range(1, chips)]
    for friend in friends:
        pl.semaphore_signal(barrier, inc=1, device_id=friend, device_id_type=MESH)

    def sib_copy(step, q, distance):
        return pltpu.make_async_remote_copy(
            src_ref=sib_send.at[step, q, distance], dst_ref=sib_recv.at[step, q, distance],
            send_sem=sib_ss.at[step, q, distance], recv_sem=sib_rs.at[step, q, distance],
            device_id=sibling, device_id_type=MESH,
        )

    def strip(piece):
        return pl.ds(piece * piece_rows, piece_rows)

    def far_copy(step, q, distance, piece):
        place = (step, q, distance - 1)
        return pltpu.make_async_remote_copy(
            src_ref=far_send.at[(*place, strip(piece))],
            dst_ref=far_recv.at[(*place, strip(piece))],
            send_sem=far_ss.at[(*place, piece)],
            recv_sem=far_rs.at[(*place, piece)],
            device_id=far_device(distance), device_id_type=MESH,
        )

    def next_copy(q, piece):
        return pltpu.make_async_remote_copy(
            src_ref=next_send.at[q, strip(piece)], dst_ref=next_recv.at[q, strip(piece)],
            send_sem=next_ss.at[q, piece], recv_sem=next_rs.at[q, piece],
            device_id=after, device_id_type=MESH,
        )

    def out_copy(piece):
        here = pl.ds(piece * out_rows, out_rows)
        return pltpu.make_async_copy(out_ref.at[here], out_hbm.at[here], out_sem.at[piece])

    def load_matrix(step, from_tile, count):
        base = lax.rem(start_ref[0] + step, steps) * (rows * tiles * 2)

        def one(turn, carry):
            tile = lax.rem(from_tile + turn, tiles)
            first = base + tile * 2
            real = factor_ref[pl.ds(first, rows, stride=tiles * 2), :]
            imag = factor_ref[pl.ds(first + 1, rows, stride=tiles * 2), :]
            high, low = split(jnp.concatenate([real, imag], 0).T)
            here = pl.ds(pl.multiple_of(tile * LANES, LANES), LANES)
            matrix[step, here, 0:2 * rows] = high
            matrix[step, here, depth:depth + 2 * rows] = high
            matrix[step, here, 2 * depth:2 * depth + 2 * rows] = low
            return carry

        lax.fori_loop(0, count, one, 0)

    def propagator(step):
        layer_id = lax.rem(start_ref[0] + step, steps)
        index = harm * rows + lax.broadcasted_iota(jnp.int32, (1, rows), 1)
        live = (index < kept_ref[layer_id]).astype(jnp.float32)
        magnitude = decay_ref[pl.ds(layer_id, 1), :] * live
        angles = phase_ref[pl.ds(layer_id, 1), :]
        for part, line in enumerate((magnitude * jnp.cos(angles), magnitude * jnp.sin(angles))):
            prop[step, part] = jnp.broadcast_to(line, (LANES, rows)).T

    def load_right(step, real, imag):
        prop_real, prop_imag = prop[step, 0], prop[step, 1]
        high_r, low_r = split(prop_real * real - prop_imag * imag)
        high_i, low_i = split(prop_real * imag + prop_imag * real)
        for place, r, i in ((0, high_r, high_i), (depth, low_r, low_i), (2 * depth, high_r, high_i)):
            right[place:place + rows, 0:LANES] = r
            right[place:place + rows, LANES:width] = i
            right[place + rows:place + 2 * rows, 0:LANES] = -i
            right[place + rows:place + 2 * rows, LANES:width] = r

    def product(step, index):
        here = pl.ds(pl.multiple_of(index * rows, rows), rows)
        return jnp.dot(matrix[step, here, :], right[...], preferred_element_type=jnp.float32)

    def give(step, q, distance):
        sib_send[step, q, distance] = product(step, far_chip(distance) * CORES + other)
        sib_copy(step, q, distance).start()

    def far_products(step, q):
        def one(distance, carry):
            give(step, q, distance)
            own[distance - 1] = product(step, far_chip(distance) * CORES + core)
            return carry

        lax.fori_loop(1, chips, one, 0)

    def far_sums(step, q):
        for distance in range(1, chips):
            sib_copy(step, q, distance).wait_recv()
            far_send[step, q, distance - 1] = own[distance - 1] + sib_recv[step, q, distance]
            for piece in range(pieces):
                far_copy(step, q, distance, piece).start()

    def hold(step, q):
        keep[step, q] = product(step, harm)

    def contribute(step, q):
        far_products(step, q)
        give(step, q, 0)
        far_sums(step, q)
        hold(step, q)

    def load_panel(q):
        first = q * 2
        load_right(
            0,
            panel_ref[pl.ds(first, rows, stride=chunks * 2), :],
            panel_ref[pl.ds(first + 1, rows, stride=chunks * 2), :],
        )

    if depth > 2 * rows:
        matrix[...] = jnp.zeros_like(matrix)
        right[...] = jnp.zeros_like(right)

    for step in range(steps):
        propagator(step)
    panel_copy.wait()
    load_panel(0)
    for copy in factor_copies:
        copy.wait()
    near = CORES * rows // LANES if CORES * rows % LANES == 0 else 0
    load_matrix(0, far_chip(1) * near, tiles - near)
    pl.semaphore_wait(barrier, len(friends))

    far_products(0, 0)
    load_matrix(0, chip * near, near)
    far_sums(0, 0)
    give(0, 0, 0)
    hold(0, 0)

    def enter(q, carry):
        load_panel(q)
        contribute(0, q)
        return carry

    lax.fori_loop(1, chunks, enter, 0)

    for step in range(1, steps):
        load_matrix(step, 0, tiles)

        def advance(q, carry, step=step):
            sib_copy(step - 1, q, 0).wait_recv()
            total = keep[step - 1, q] + sib_recv[step - 1, q, 0]
            for distance in range(1, chips):
                for piece in range(pieces):
                    far_copy(step - 1, q, distance, piece).wait_recv()
                total = total + far_recv[step - 1, q, distance - 1]
            load_right(step, total[:, 0:LANES], total[:, LANES:width])
            contribute(step, q)
            return carry

        lax.fori_loop(0, chunks, advance, 0)

    last = steps - 1

    def leave(q, carry):
        sib_copy(last, q, 0).wait_recv()
        for piece in range(pieces):
            here = strip(piece)
            total = keep[last, q, here] + sib_recv[last, q, 0, here]
            for distance in range(1, chips):
                far_copy(last, q, distance, piece).wait_recv()
                total = total + far_recv[last, q, distance - 1, here]
            next_send[q, here] = total
            next_copy(q, piece).start()
        return carry

    lax.fori_loop(0, chunks, leave, 0)

    for q in range(chunks):
        for piece in range(pieces):
            next_copy(q, piece).wait_recv()
            for part in range(2):
                there = pl.ds(piece * out_rows + q * 2 + part, piece_rows, stride=chunks * 2)
                out_ref[there, :] = next_recv[q, strip(piece), part * LANES:(part + 1) * LANES]
            if q == chunks - 1:
                out_copy(piece).start()

    def finish(q, carry):
        for step in range(steps):
            for distance in range(chips):
                sib_copy(step, q, distance).wait_send()
            for distance in range(1, chips):
                for piece in range(pieces):
                    far_copy(step, q, distance, piece).wait_send()
        for piece in range(pieces):
            next_copy(q, piece).wait_send()
        return carry

    lax.fori_loop(0, chunks, finish, 0)
    for piece in range(pieces):
        out_copy(piece).wait()


def lines(array):
    lead = array.shape[:-1]
    tiles = array.shape[-1] // LANES
    split_up = array.reshape(-1, lead[-1], tiles, LANES)
    split_up = with_layout_constraint(split_up, Layout(major_to_minor=(0, 2, 1, 3)))
    return split_up.transpose(0, 2, 1, 3).reshape(-1, LANES)


def on_device(panels, factors, decay, phase, kept, start):
    steps, rows, _, harmonics = factors.shape
    columns = panels.shape[-1]
    chips = lax.axis_size("harm") // CORES
    groups = lax.axis_size("layer")
    chunks = columns // LANES
    depth = -(-2 * rows // LANES) * LANES
    width = 2 * LANES

    pieces = next(count for count in (5, 4, 2, 1) if rows % (8 * count) == 0)
    vmem = pl.BlockSpec(memory_space=pltpu.VMEM)
    smem = pl.BlockSpec(memory_space=pltpu.SMEM)
    hbm = pl.BlockSpec(memory_space=pl.ANY)
    dma = pltpu.SemaphoreType.DMA
    far = max(chips - 1, 1)
    panel_lines, factor_lines = lines(panels), lines(factors)
    result = pl.pallas_call(
        functools.partial(kernel, steps, chips, groups, rows, harmonics, chunks, depth, pieces),
        out_shape=jax.ShapeDtypeStruct(panel_lines.shape, jnp.float32),
        in_specs=[smem, smem, vmem, vmem, hbm, hbm],
        out_specs=hbm,
        scratch_shapes=[
            pltpu.VMEM(panel_lines.shape, jnp.float32),
            pltpu.VMEM(factor_lines.shape, jnp.float32),
            pltpu.VMEM(panel_lines.shape, jnp.float32),
            pltpu.VMEM((steps, harmonics, 3 * depth), jnp.bfloat16),
            pltpu.VMEM((3 * depth, width), jnp.bfloat16),
            pltpu.VMEM((steps, 2, rows, LANES), jnp.float32),
            pltpu.VMEM((far, rows, width), jnp.float32),
            pltpu.VMEM((steps, chunks, chips, rows, width), jnp.float32),
            pltpu.VMEM((steps, chunks, chips, rows, width), jnp.float32),
            pltpu.VMEM((steps, chunks, rows, width), jnp.float32),
            pltpu.VMEM((steps, chunks, far, rows, width), jnp.float32),
            pltpu.VMEM((steps, chunks, far, rows, width), jnp.float32),
            pltpu.VMEM((chunks, rows, width), jnp.float32),
            pltpu.VMEM((chunks, rows, width), jnp.float32),
            dma((1 + steps,)),
            dma((pieces,)),
            dma((steps, chunks, chips)),
            dma((steps, chunks, chips)),
            dma((steps, chunks, far, pieces)),
            dma((steps, chunks, far, pieces)),
            dma((chunks, pieces)),
            dma((chunks, pieces)),
        ],
        compiler_params=pltpu.CompilerParams(
            collective_id=0, has_side_effects=True, vmem_limit_bytes=60 * 2**20
        ),
    )(start, kept, decay, phase, panel_lines, factor_lines)
    result = result.reshape(rows, chunks, 2, LANES).transpose(0, 2, 1, 3)
    result = with_layout_constraint(result, Layout(major_to_minor=(0, 2, 1, 3)))
    return result.reshape(panels.shape)


def solution(mesh):
    in_specs = (
        P(("grating", "layer"), "harm", None, None),
        P(("grating", "layer"), "harm", None, None),
        P(("grating", "layer"), "harm"),
        P(("grating", "layer"), "harm"),
        P(("grating", "layer")),
        P(("grating", "layer")),
    )
    out_specs = P(("grating", "layer"), "harm", None, None)
    return jax.shard_map(
        on_device, mesh=mesh, in_specs=in_specs, out_specs=out_specs, check_vma=False
    )
```

time: 101 us -> 96.5 us (0.955)
  Pallas kernels: 96.1 us -> 92.5 us
    reshape x2 -> x0, local copies, waits for them, and re-layouts: 3.82 us -> none  [on_device(): result = result.reshape(chunks, rows, 2, LANES).transpose(1, 2, 0, 3)]
    pallas_call x1, Pallas kernels: 96.1 us -> 92.5 us  [on_device(): pl.pallas_call(functools.partial(kernel, steps, chips, groups, rows, harm...]
    unnamed x0 -> x1, local copies, waits for them, and re-layouts: none -> 3.16 us
where the time goes in v2:
time: 96.5 us; the launch traced here: 96.3 us
  Pallas kernels  92.5 us (96%)
  local copies, waits for them, and re-layouts  3.16 us (3%)
    pallas_call x1, Pallas kernels, on_device(): pl.pallas_call(functools.partial(kernel, steps, chips, groups, rows, harm...  92.5 us
    unnamed x1, local copies, waits for them, and re-layouts  3.16 us

profile of v2, /device:TPU:0, one launch (start us, length us, event | category | flops | bytes accessed | tf_op | source)
XLA Modules:
  0.0 96.3 jit_solution(8798327758392478258)
XLA Ops:
  0.7 92.5 %shard_map.64 = f32[3200,128]{1,0:T(8,128)} custom-call(s32[1]{0:T(128)S(6)} %copy.8.start_ref, s32[2]{0:T(128)} %kept_ref.1, f32[2,320]{1,0:T(2,128)} %decay_ref.1, f32[2,320]{1,0:T(2,128)} %phase_ref.1, f32[3200,128]{1,0:T(8,128)} %bitcast.17, f32[12800,128]{1,0:T(8,128)} %bitcast.15), custom_call_target="tpu_custom_call" | custom-call | tf_op jit(solution)/shard_map/pallas_call | solution.py:281
  93.2 3.2 %copy.9 = f32[1,320,2,640]{3,2,1,0:T(2,128)} copy(f32[1,320,2,640]{3,2,1,0:T(2,128)} %bitcast.16) | data formatting | bytes 3276800

commit v3 on v2

--- a/solution.py
+++ b/solution.py
@@ -70,14 +70,17 @@
             device_id=sibling, device_id_type=MESH,
         )
 
-    def strip(piece):
-        return pl.ds(piece * piece_rows, piece_rows)
+    def cuts(step):
+        return pieces if step == steps - 1 else 1
+
+    def strip(piece, count=pieces):
+        return pl.ds(piece * (rows // count), rows // count)
 
     def far_copy(step, q, distance, piece):
         place = (step, q, distance - 1)
         return pltpu.make_async_remote_copy(
-            src_ref=far_send.at[(*place, strip(piece))],
-            dst_ref=far_recv.at[(*place, strip(piece))],
+            src_ref=far_send.at[(*place, strip(piece, cuts(step)))],
+            dst_ref=far_recv.at[(*place, strip(piece, cuts(step)))],
             send_sem=far_ss.at[(*place, piece)],
             recv_sem=far_rs.at[(*place, piece)],
             device_id=far_device(distance), device_id_type=MESH,
@@ -149,8 +152,11 @@
     def far_sums(step, q):
         for distance in range(1, chips):
             sib_copy(step, q, distance).wait_recv()
-            far_send[step, q, distance - 1] = own[distance - 1] + sib_recv[step, q, distance]
-            for piece in range(pieces):
+            for piece in range(cuts(step)):
+                here = strip(piece, cuts(step))
+                far_send[step, q, distance - 1, here] = (
+                    own[distance - 1, here] + sib_recv[step, q, distance, here]
+                )
                 far_copy(step, q, distance, piece).start()
 
     def hold(step, q):
@@ -185,8 +191,8 @@
     pl.semaphore_wait(barrier, len(friends))
 
     far_products(0, 0)
+    far_sums(0, 0)
     load_matrix(0, chip * near, near)
-    far_sums(0, 0)
     give(0, 0, 0)
     hold(0, 0)
 
@@ -204,7 +210,7 @@
             sib_copy(step - 1, q, 0).wait_recv()
             total = keep[step - 1, q] + sib_recv[step - 1, q, 0]
             for distance in range(1, chips):
-                for piece in range(pieces):
+                for piece in range(cuts(step - 1)):
                     far_copy(step - 1, q, distance, piece).wait_recv()
                 total = total + far_recv[step - 1, q, distance - 1]
             load_right(step, total[:, 0:LANES], total[:, LANES:width])
@@ -243,7 +249,7 @@
             for distance in range(chips):
                 sib_copy(step, q, distance).wait_send()
             for distance in range(1, chips):
-                for piece in range(pieces):
+                for piece in range(cuts(step)):
                     far_copy(step, q, distance, piece).wait_send()
         for piece in range(pieces):
             next_copy(q, piece).wait_send()
@@ -271,7 +277,7 @@
     depth = -(-2 * rows // LANES) * LANES
     width = 2 * LANES
 
-    pieces = next(count for count in (5, 4, 2, 1) if rows % (8 * count) == 0)
+    pieces = next(count for count in (2, 1) if rows % (8 * count) == 0)
     vmem = pl.BlockSpec(memory_space=pltpu.VMEM)
     smem = pl.BlockSpec(memory_space=pltpu.SMEM)
     hbm = pl.BlockSpec(memory_space=pl.ANY)

time: 96.5 us -> 95.5 us (0.990)
  Pallas kernels: 92.5 us -> 91.5 us
    pallas_call x1, Pallas kernels: 92.5 us -> 91.5 us  [on_device(): pl.pallas_call(functools.partial(kernel, steps, chips, groups, rows, harm...]
where the time goes in v3:
time: 95.5 us; the launch traced here: 95.3 us
  Pallas kernels  91.5 us (96%)
  local copies, waits for them, and re-layouts  3.16 us (3%)
    pallas_call x1, Pallas kernels, on_device(): pl.pallas_call(functools.partial(kernel, steps, chips, groups, rows, harm...  91.5 us
    unnamed x1, local copies, waits for them, and re-layouts  3.16 us

profile of v3, /device:TPU:0, one launch (start us, length us, event | category | flops | bytes accessed | tf_op | source)
XLA Modules:
  0.0 95.3 jit_solution(11400812909529357714)
XLA Ops:
  0.7 91.5 %shard_map.64 = f32[3200,128]{1,0:T(8,128)} custom-call(s32[1]{0:T(128)S(6)} %copy.8.start_ref, s32[2]{0:T(128)} %kept_ref.1, f32[2,320]{1,0:T(2,128)} %decay_ref.1, f32[2,320]{1,0:T(2,128)} %phase_ref.1, f32[3200,128]{1,0:T(8,128)} %bitcast.17, f32[12800,128]{1,0:T(8,128)} %bitcast.15), custom_call_target="tpu_custom_call" | custom-call | tf_op jit(solution)/shard_map/pallas_call | solution.py:287
  92.1 3.2 %copy.9 = f32[1,320,2,640]{3,2,1,0:T(2,128)} copy(f32[1,320,2,640]{3,2,1,0:T(2,128)} %bitcast.16) | data formatting | bytes 3276800
